TPU v7x, 256 devices: a whole 4x4x8 slice. The times are simulated.
256 devices in a mesh: seq: 32 (over z, x_hi, core), fsdp: 8 (over y, x_lo).
Axes of the slice: x: 4 (x_hi: 2, x_lo: 2; x = x_hi * 2 + x_lo), y: 4, z: 8, core: 2. Of those that a mesh axis runs over, the one named last changes fastest.
Arguments:
- queries: bfloat16 [8, 4096, 2048], P('fsdp', 'seq'), may hold values from -6 to 6
- key_vectors: bfloat16 [8, 4096, 2048], P('fsdp', 'seq'), may hold values from -6 to 6
- value_vectors: bfloat16 [8, 4096, 2048], P('fsdp', 'seq'), may hold values from -6 to 6
- out_grad: bfloat16 [8, 4096, 2048], P('fsdp', 'seq'), may hold values from -6 to 6
- out_weight: bfloat16 [2048, 2048], P(None, 'fsdp'), may hold values from -0.125 to 0.125
Outputs:
- query_grad: bfloat16 [8, 4096, 2048], P('fsdp', 'seq')
- key_grad: bfloat16 [8, 4096, 2048], P('fsdp', 'seq')
- value_grad: bfloat16 [8, 4096, 2048], P('fsdp', 'seq')
- weight_grad: float32 [2048, 2048], P('seq', 'fsdp')
All inputs are finite; a program needn't handle non-finite values.
Results may differ from a plain program's by a relative error of at most 0.005.
Values may be sent and summed in bfloat16 or wider, within the bound.
A program may use at most 192 MiB of HBM per device.

v0:
```python
import math
import jax
import jax.numpy as jnp
from jax import lax
from jax.sharding import PartitionSpec as P

HEADS = 16
HEAD_DIM = 128
BLOCK = 128


def carried_in(value, axis, combine, identity, reverse):
    length, here = (lax.axis_size(axis), lax.axis_index(axis))
    everything = lax.all_gather(value, axis)
    start = jnp.broadcast_to(jnp.asarray(identity, value.dtype), value.shape)

    def lap(k, before):
        at = length - 1 - k if reverse else k
        reached = at > here if reverse else at < here
        new = combine(before, everything[at])
        return jnp.where(reached, new, before)

    return lax.fori_loop(0, length, lap, start)


def add_states(earlier, after_dev):
    return earlier + after_dev


def attend(queries, key_vectors, value_vectors, grads, factor):
    batches, tokens, head_count, head_width = queries.shape
    blocks = tokens // BLOCK
    shape_five = (batches, blocks, BLOCK, head_count, head_width)
    query_wide = queries.reshape(shape_five)
    keys_wide = key_vectors.reshape(shape_five)
    values_wide = value_vectors.reshape(shape_five)
    grads_wide = grads.reshape(shape_five)
    single = jnp.float32
    higher = lax.Precision.HIGH
    key_value = jnp.einsum(
        "bnshd,bnshe->bnhde", keys_wide, values_wide, preferred_element_type=single
    )
    query_cot = jnp.einsum(
        "bnthd,bnthe->bnhde", query_wide, grads_wide, preferred_element_type=single
    )
    key_value_dev = jnp.sum(key_value, 1)
    query_cot_dev = jnp.sum(query_cot, 1)
    nothing = jnp.zeros_like(key_value_dev)
    earlier = carried_in(key_value_dev, "seq", add_states, nothing, False)
    after_dev = carried_in(query_cot_dev, "seq", add_states, nothing, True)
    s_before = earlier[:, None] + jnp.cumsum(key_value, 1) - key_value
    g_after = after_dev[:, None] + query_cot_dev[:, None] - jnp.cumsum(query_cot, 1)
    row_index = lax.broadcasted_iota(jnp.int32, (BLOCK, BLOCK), 0)
    col_index = lax.broadcasted_iota(jnp.int32, (BLOCK, BLOCK), 1)
    causal = (row_index >= col_index).astype(jnp.float32)
    scores = jnp.einsum("bnthd,bnshd->bnhts", query_wide, keys_wide, preferred_element_type=single)
    scores = (scores * causal).astype(jnp.bfloat16)
    mixing = jnp.einsum(
        "bnthe,bnshe->bnhts", grads_wide, values_wide, preferred_element_type=single
    )
    mixing = (mixing * causal).astype(jnp.bfloat16)
    attended = jnp.einsum(
        "bnthd,bnhde->bnthe", query_wide.astype(single), s_before, precision=higher
    )
    attended = attended + jnp.einsum(
        "bnhts,bnshe->bnthe", scores, values_wide, preferred_element_type=single
    )
    query_grad = jnp.einsum(
        "bnthe,bnhde->bnthd", grads_wide.astype(single), s_before, precision=higher
    )
    query_grad = query_grad + jnp.einsum(
        "bnhts,bnshd->bnthd", mixing, keys_wide, preferred_element_type=single
    )
    key_grad = jnp.einsum(
        "bnshe,bnhde->bnshd", values_wide.astype(single), g_after, precision=higher
    )
    key_grad = key_grad + jnp.einsum(
        "bnhts,bnthd->bnshd", mixing, query_wide, preferred_element_type=single
    )
    value_grad = jnp.einsum(
        "bnshd,bnhde->bnshe", keys_wide.astype(single), g_after, precision=higher
    )
    value_grad = value_grad + jnp.einsum(
        "bnhts,bnthe->bnshe", scores, grads_wide, preferred_element_type=single
    )
    flat = (batches, tokens, head_count * head_width)
    return (
        factor * attended.reshape(flat),
        factor * query_grad.reshape(flat),
        factor * key_grad.reshape(flat),
        factor * value_grad.reshape(flat),
    )


def split_heads(values_in, head_count):
    return values_in.reshape(values_in.shape[0], values_in.shape[1], head_count, HEAD_DIM)


def body(queries, key_vectors, value_vectors, out_grad, out_weight):
    seq_devices = lax.axis_size("seq")
    fsdp_devices = lax.axis_size("fsdp")
    tokens = queries.shape[1]
    factor = 1.0 / math.sqrt(HEAD_DIM * tokens * seq_devices)
    grad_factor = 1.0 / math.sqrt(fsdp_devices * tokens * seq_devices)
    group_count = HEADS // fsdp_devices
    grads_all = lax.all_gather(out_grad, "fsdp", axis=0, tiled=True)
    grad_attn = jnp.einsum(
        "btd,dc->btc", grads_all, out_weight, preferred_element_type=jnp.float32
    ).astype(jnp.bfloat16)
    moved = (
        lax.all_to_all(queries, "fsdp", split_axis=2, concat_axis=0, tiled=True),
        lax.all_to_all(key_vectors, "fsdp", split_axis=2, concat_axis=0, tiled=True),
        lax.all_to_all(value_vectors, "fsdp", split_axis=2, concat_axis=0, tiled=True),
    )
    attended, query_grad, key_grad, value_grad = attend(
        split_heads(moved[0], group_count),
        split_heads(moved[1], group_count),
        split_heads(moved[2], group_count),
        split_heads(grad_attn, group_count),
        factor,
    )
    returned = (
        lax.all_to_all(
            query_grad.astype(jnp.bfloat16), "fsdp", split_axis=0, concat_axis=2, tiled=True
        ),
        lax.all_to_all(
            key_grad.astype(jnp.bfloat16), "fsdp", split_axis=0, concat_axis=2, tiled=True
        ),
        lax.all_to_all(
            value_grad.astype(jnp.bfloat16), "fsdp", split_axis=0, concat_axis=2, tiled=True
        ),
    )
    attended_low = attended.astype(jnp.bfloat16)
    weight_grad = (
        lax.psum_scatter(
            lax.dot_general(
                grads_all,
                attended_low,
                (((0, 1), (0, 1)), ((), ())),
                preferred_element_type=jnp.float32,
            ),
            "seq",
            scatter_dimension=0,
            tiled=True,
        )
        * grad_factor
    )
    return (returned[0], returned[1], returned[2], weight_grad)


def solution(mesh):
    in_specs = (
        P("fsdp", "seq", None),
        P("fsdp", "seq", None),
        P("fsdp", "seq", None),
        P("fsdp", "seq", None),
        P(None, "fsdp"),
    )
    out_specs = (
        P("fsdp", "seq", None),
        P("fsdp", "seq", None),
        P("fsdp", "seq", None),
        P("seq", "fsdp"),
    )
    return jax.shard_map(body, mesh=mesh, in_specs=in_specs, out_specs=out_specs, check_vma=False)
```

profile of v0, /device:TPU:8, one launch (start us, length us, event | category | flops | bytes accessed | tf_op | source)
XLA Modules:
  0.0 716.8 jit_solution(7374934269452240862)
XLA Ops:
  7.9 2.4 copy.72
  10.8 11.5 %reduce = bf16[2048,128]{1,0:T(8,128)(2,1)S(1)} reduce(bf16[2048,1,128]{2,1,0:T(2,128)(2,1)S(1)} %bitcast.143, bf16[]{:T(256)} %broadcast.48), dimensions={1}, to_apply=%bitcast.91.reduce_sub_computation | reduce | bytes 1048578
  23.2 5.8 all-to-all-start
  29.1 2.3 copy.73
  31.4 11.5 %reduce.1 = bf16[2048,128]{1,0:T(8,128)(2,1)S(1)} reduce(bf16[2048,1,128]{2,1,0:T(2,128)(2,1)S(1)} %bitcast.145, bf16[]{:T(256)} %broadcast.48), dimensions={1}, to_apply=%bitcast.93.reduce_sub_computation | reduce | bytes 1048578
  43.9 5.9 all-to-all-start.1
  50.4 13.2 %all-to-all-done.1 = bf16[8,2,16384]{2,1,0:T(2,128)(2,1)} async-done(((bf16[8,2,16384]{2,1,0:T(2,128)(2,1)}), bf16[8,2,16384]{2,1,0:T(2,128)(2,1)}, u32[]{:S(2)}, u32[]{:S(2)}) %all-to-all-start.1) | async-done | bytes 524320 | tf_op jit(solution)/shard_map/all_to_all | solution.py:113
  63.7 2.2 reshape.158
  69.2 11.5 %reduce.2 = bf16[2048,128]{1,0:T(8,128)(2,1)S(1)} reduce(bf16[2048,1,128]{2,1,0:T(2,128)(2,1)S(1)} %bitcast.144, bf16[]{:T(256)} %broadcast.48), dimensions={1}, to_apply=%bitcast.95.reduce_sub_computation | reduce | bytes 1048578
  80.9 18.6 %all_to_all.99 = bf16[8,2,16384]{2,1,0:T(2,128)(2,1)S(1)} all-to-all(bf16[8,2,16384]{2,1,0:T(2,128)(2,1)S(1)} %reshape.159), channel_id=1, replica_groups=mesh['seq'=32,'fsdp'=8] {'fsdp'}, dimensions={0} | all-to-all | bytes 1048576 | tf_op jit(solution)/shard_map/all_to_all | solution.py:111
  100.2 21.6 %all-gather.6.cloned.1.call-done = bf16[8,128,2048]{2,1,0:T(8,128)(2,1)} async-done(((bf16[1,128,2048]{2,1,0:T(8,128)(2,1)}), bf16[8,128,2048]{2,1,0:T(8,128)(2,1)}) %all-gather.6.cloned.1.call-update) | async-done | bytes 4194320 | tf_op jit(solution)/shard_map/all_gather | solution.py:106
  121.7 3.4 convolution_convert_fusion
  127.4 2.3 fusion.12
  129.7 2.3 fusion.11
  132.0 220.7 %all-gather.8.cloned.1.call-done = f32[256,2,128,128]{3,2,1,0:T(8,128)} async-done(((f32[8,2,128,128]{3,2,1,0:T(8,128)}), f32[256,2,128,128]{3,2,1,0:T(8,128)}) %all-gather.8.cloned.1.call-update) | async-done | bytes 33554448 | tf_op jit(solution)/shard_map/all_gather | solution.py:14
  352.8 51.9 %while.30 = (s32[]{:T(128)}, f32[8,2,128,128]{3,2,1,0:T(8,128)S(1)}, s32[]{:T(128)}, f32[32,8,2,128,128]{4,3,2,1,0:T(8,128)}, s32[]{:T(128)}, /*index=5*/s32[]{:T(128)}) while((s32[]{:T(128)}, f32[8,2,128,128]{3,2,1,0:T(8,128)S(1)}, s32[]{:T(128)}, f32[32,8,2,128,128]{4,3,2,1,0:T(8,128)}, s32[]{:T(128)}, /*index=5*/s32[]{:T(128)}) %tuple.92), condition=%wide.region_1.0_spmd.clone, body=%wide.region_0.0_spmd.clone.sunk | while | flops 786436 | bytes 3145821 | solution.py:23
  404.7 2.3 fusion.14
  408.7 2.6 convolution_bitcast_fusion
  411.4 2.9 copy.108
  416.0 2.5 fusion.7
  418.5 5.1 all-to-all-start.2
  424.2 159.7 %all-gather.10.cloned.1.call-done = f32[256,2,128,128]{3,2,1,0:T(8,128)} async-done(((f32[8,2,128,128]{3,2,1,0:T(8,128)}), f32[256,2,128,128]{3,2,1,0:T(8,128)}) %all-gather.10.cloned.1.call-update) | async-done | bytes 33554448 | tf_op jit(solution)/shard_map/all_gather | solution.py:14
  583.9 52.1 %while.31 = (s32[]{:T(128)}, f32[8,2,128,128]{3,2,1,0:T(8,128)S(1)}, s32[]{:T(128)}, f32[32,8,2,128,128]{4,3,2,1,0:T(8,128)}, s32[]{:T(128)}, /*index=5*/s32[]{:T(128)}, s32[]{:T(128)}, s32[]{:T(128)}) while((s32[]{:T(128)}, f32[8,2,128,128]{3,2,1,0:T(8,128)S(1)}, s32[]{:T(128)}, f32[32,8,2,128,128]{4,3,2,1,0:T(8,128)}, s32[]{:T(128)}, ...), condition=%wide.region_3.4_spmd.clone, body=%wide.region_2.3_spmd.clone.sunk | while | flops 786440 | bytes 3145883 | solution.py:23
  639.1 2.3 fusion.8
  641.5 5.1 all-to-all-start.5
  646.6 2.0 fusion.17
  648.7 2.1 fusion.10
  650.8 4.3 all-to-all-done.5
  655.1 5.5 all-to-all-start.4
  660.6 2.0 copy.105
  662.6 42.9 %reduce-scatter.4.cloned.1.call-done = f32[64,256]{1,0:T(8,128)} async-done(((f32[2048,256]{1,0:T(8,128)}), f32[64,256]{1,0:T(8,128)}) %reduce-scatter.4.cloned.1.call-update) | async-done | bytes 65552
  707.2 2.0 copy.107
  (122 shorter events, 122.0 us)
Async XLA Ops:
  7.2 114.6 %copy-start = (bf16[2048,256]{1,0:T(8,128)(2,1)S(1)}, bf16[2048,256]{1,0:T(8,128)(2,1)}, u32[]{:S(2)}) copy-start(bf16[2048,256]{1,0:T(8,128)(2,1)} %param.13) | copy-start | bytes 3145732
  7.2 114.6 %all-gather.6.cloned.1.call-start = ((), (), s32[]{:S(2)}) async-start(), calls=%async_computation.7 | async-start | bytes 4718592 | tf_op jit(solution)/shard_map/all_gather | solution.py:106
  23.2 20.6 %all-to-all-start = ((bf16[8,2,16384]{2,1,0:T(2,128)(2,1)}), bf16[8,2,16384]{2,1,0:T(2,128)(2,1)S(1)}, u32[]{:S(2)}, u32[]{:S(2)}) async-start(bf16[8,2,16384]{2,1,0:T(2,128)(2,1)} %reshape.155), calls=%async_computation | async-start | bytes 1048576 | tf_op jit(solution)/shard_map/all_to_all | solution.py:112
  43.9 19.8 %all-to-all-start.1 = ((bf16[8,2,16384]{2,1,0:T(2,128)(2,1)}), bf16[8,2,16384]{2,1,0:T(2,128)(2,1)}, u32[]{:S(2)}, u32[]{:S(2)}) async-start(bf16[8,2,16384]{2,1,0:T(2,128)(2,1)} %reshape.157), calls=%async_computation.1 | async-start | bytes 1048576 | tf_op jit(solution)/shard_map/all_to_all | solution.py:113
  49.8 303.0 %all-gather.8.cloned.1.call-start = ((), (), s32[]{:S(2)}) async-start(), calls=%async_computation.8 | async-start | bytes 34603008 | tf_op jit(solution)/shard_map/all_gather | solution.py:14
  50.3 18.1 %copy-start.9 = (bf16[1,128,2048]{2,1,0:T(8,128)(2,1)S(1)}, bf16[1,128,2048]{2,1,0:T(8,128)(2,1)}, u32[]{:S(2)}) copy-start(bf16[1,128,2048]{2,1,0:T(8,128)(2,1)} %param.9) | copy-start | bytes 1572868
  50.4 30.4 %copy-start.4 = (bf16[1,128,2048]{1,2,0:T(8,128)(2,1)}, bf16[1,128,2048]{1,2,0:T(8,128)(2,1)S(1)}, u32[]{:S(2)}) copy-start(bf16[1,128,2048]{1,2,0:T(8,128)(2,1)S(1)} %copy.110) | copy-start | bytes 1572868
  66.0 0.8 copy-start.2
  68.2 515.7 %all-gather.10.cloned.1.call-start = ((), (), s32[]{:S(2)}) async-start(), calls=%async_computation.9 | async-start | bytes 34603008 | tf_op jit(solution)/shard_map/all_gather | solution.py:14
  100.2 25.3 %copy-start.6 = (bf16[1,128,2048]{1,2,0:T(8,128)(2,1)}, bf16[1,128,2048]{1,2,0:T(8,128)(2,1)S(1)}, u32[]{:S(2)}) copy-start(bf16[1,128,2048]{1,2,0:T(8,128)(2,1)S(1)} %copy.112) | copy-start | bytes 1572868
  125.5 1.9 copy-start.8
  404.7 4.0 copy-start.10
  418.5 222.9 %all-to-all-start.2 = ((bf16[8,128,256]{1,2,0:T(8,128)(2,1)}), bf16[8,128,256]{1,2,0:T(8,128)(2,1)}, u32[]{:S(2)}, u32[]{:S(2)}) async-start(bf16[8,128,256]{1,2,0:T(8,128)(2,1)} %bitcast.11), calls=%async_computation.2 | async-start | bytes 1048576 | tf_op jit(solution)/shard_map/all_to_all | solution.py:123
  423.6 281.9 %reduce-scatter.4.cloned.1.call-start = ((), (), s32[]{:S(2)}) async-start(), calls=%async_computation.10 | async-start | bytes 2162688
  583.9 53.5 %copy-start.5 = (bf16[1,128,2048]{1,2,0:T(8,128)(2,1)S(1)}, bf16[1,128,2048]{1,2,0:T(8,128)(2,1)}, u32[]{:S(2)}) copy-start(bf16[1,128,2048]{1,2,0:T(8,128)(2,1)} %copy-done.4) | copy-start | bytes 1572868
  637.4 9.2 %copy-start.3 = (bf16[1,128,2048]{1,2,0:T(8,128)(2,1)S(1)}, bf16[1,128,2048]{1,2,0:T(8,128)(2,1)}, u32[]{:S(2)}) copy-start(bf16[1,128,2048]{1,2,0:T(8,128)(2,1)} %copy-done.2) | copy-start | bytes 1572868
  639.1 9.5 %copy-start.7 = (bf16[1,128,2048]{1,2,0:T(8,128)(2,1)S(1)}, bf16[1,128,2048]{1,2,0:T(8,128)(2,1)}, u32[]{:S(2)}) copy-start(bf16[1,128,2048]{1,2,0:T(8,128)(2,1)} %copy-done.6) | copy-start | bytes 1572868
  641.5 13.6 %all-to-all-start.5 = ((bf16[8,128,256]{1,2,0:T(8,128)(2,1)}), bf16[8,128,256]{1,2,0:T(8,128)(2,1)}, u32[]{:S(2)}, u32[]{:S(2)}) async-start(bf16[8,128,256]{1,2,0:T(8,128)(2,1)} %bitcast.146), calls=%async_computation.5 | async-start | bytes 1048576 | tf_op jit(solution)/shard_map/all_to_all | solution.py:129
  646.6 63.7 %copy-start.1 = (bf16[2048,256]{1,0:T(8,128)(2,1)S(1)}, bf16[2048,256]{1,0:T(8,128)(2,1)}, u32[]{:S(2)}) copy-start(bf16[2048,256]{1,0:T(8,128)(2,1)} %param.13) | copy-start | bytes 3145732
  655.1 54.1 %all-to-all-start.4 = ((bf16[8,128,256]{1,2,0:T(8,128)(2,1)}), bf16[8,128,256]{1,2,0:T(8,128)(2,1)S(1)}, u32[]{:S(2)}, u32[]{:S(2)}) async-start(bf16[8,128,256]{1,2,0:T(8,128)(2,1)} %bitcast.23), calls=%async_computation.4 | async-start | bytes 1048576 | tf_op jit(solution)/shard_map/all_to_all | solution.py:126
Sparse Core Ops, SparseCore 0:
  9.8 111.9 all-gather.5
  124.5 228.2 all-gather.7
  355.6 228.2 all-gather.9
  587.9 117.6 reduce-scatter.3
where the time goes:
time: 720 us; the launch traced here: 717 us
  waiting for transfers between devices  464 us (64%)
  other arithmetic  137 us (19%)
  matrix products  29.2 us (4%)
  starting transfers between devices  27.7 us (4%)
  local copies, waits for them, and re-layouts  24.8 us (3%)
  blocking collectives  18.6 us (3%)
  between operations  14.1 us (2%)
    all_gather x2, waiting for transfers between devices, carried_in(): everything = lax.all_gather(value, axis)  380 us
    select_n x64, other arithmetic, lap(): return jnp.where(reached, new, before)  102 us
    unnamed x5, waiting for transfers between devices  44.2 us
    unnamed x5, other arithmetic  34.6 us
    all_gather x1, waiting for transfers between devices, body(): grads_all = lax.all_gather(out_grad, 'fsdp', axis=0, tiled=True)  21.6 us
    all_to_all x1, blocking collectives, body(): lax.all_to_all(queries, 'fsdp', split_axis=2, concat_axis=0, tiled=True)  18.6 us
    unnamed x38, local copies, waits for them, and re-layouts  16.8 us
  transfers between devices with their start and end apart: 9, of which 6 were waited for; matrix products, arithmetic and copies ran while one was open for 26% of the time, Pallas kernels for 0%

commit v1 on v0

--- a/solution.py
+++ b/solution.py
@@ -103,7 +103,9 @@
     factor = 1.0 / math.sqrt(HEAD_DIM * tokens * seq_devices)
     grad_factor = 1.0 / math.sqrt(fsdp_devices * tokens * seq_devices)
     group_count = HEADS // fsdp_devices
-    grads_all = lax.all_gather(out_grad, "fsdp", axis=0, tiled=True)
+    grads_all = jnp.concatenate(
+        lax.all_to_all(jnp.stack([out_grad] * lax.axis_size("fsdp")), "fsdp", 0, 0), axis=0
+    )
     grad_attn = jnp.einsum(
         "btd,dc->btc", grads_all, out_weight, preferred_element_type=jnp.float32
     ).astype(jnp.bfloat16)

time: 720 us -> 673 us (0.935)
  waiting for transfers between devices: 464 us -> 404 us
    all_gather x2, waiting for transfers between devices: 380 us -> 294 us  [carried_in(): everything = lax.all_gather(value, axis)]
    all_to_all x0 -> x1, waiting for transfers between devices: none -> 55.7 us  [body(): lax.all_to_all(jnp.stack([out_grad] * lax.axis_size('fsdp')), 'fsdp', 0, 0)]
    all_gather x1 -> x0, waiting for transfers between devices: 21.6 us -> none  [body(): grads_all = lax.all_gather(out_grad, 'fsdp', axis=0, tiled=True)]
    unnamed x5 -> x4, waiting for transfers between devices: 44.2 us -> 42.5 us
    unnamed x38 -> x36, local copies, waits for them, and re-layouts: 16.8 us -> 16.8 us
where the time goes in v1:
time: 673 us; the launch traced here: 669 us
  waiting for transfers between devices  404 us (60%)
  other arithmetic  137 us (20%)
  starting transfers between devices  34.7 us (5%)
  matrix products  31.3 us (5%)
  local copies, waits for them, and re-layouts  28.4 us (4%)
  blocking collectives  17.9 us (3%)
  between operations  14 us (2%)
    all_gather x2, waiting for transfers between devices, carried_in(): everything = lax.all_gather(value, axis)  294 us
    select_n x64, other arithmetic, lap(): return jnp.where(reached, new, before)  103 us
    all_to_all x1, waiting for transfers between devices, body(): lax.all_to_all(jnp.stack([out_grad] * lax.axis_size('fsdp')), 'fsdp', 0, 0)  55.7 us
    unnamed x4, waiting for transfers between devices  42.5 us
    unnamed x5, other arithmetic  34.6 us
    all_to_all x1, blocking collectives, body(): lax.all_to_all(queries, 'fsdp', split_axis=2, concat_axis=0, tiled=True)  17.9 us
    unnamed x36, local copies, waits for them, and re-layouts  16.8 us
  transfers between devices with their start and end apart: 9, of which 6 were waited for; matrix products, arithmetic and copies ran while one was open for 26% of the time, Pallas kernels for 0%

profile of v1, /device:TPU:8, one launch (start us, length us, event | category | flops | bytes accessed | tf_op | source)
XLA Modules:
  0.0 669.4 jit_solution(4301779009085211165)
XLA Ops:
  7.2 2.4 copy.72
  10.1 11.5 %reduce = bf16[2048,128]{1,0:T(8,128)(2,1)S(1)} reduce(bf16[2048,1,128]{2,1,0:T(2,128)(2,1)S(1)} %bitcast.151, bf16[]{:T(256)} %broadcast.51), dimensions={1}, to_apply=%bitcast.101.reduce_sub_computation | reduce | bytes 1048578
  22.6 5.8 all-to-all-start
  28.4 2.3 copy.73
  30.8 11.5 %reduce.1 = bf16[2048,128]{1,0:T(8,128)(2,1)S(1)} reduce(bf16[2048,1,128]{2,1,0:T(2,128)(2,1)S(1)} %bitcast.153, bf16[]{:T(256)} %broadcast.51), dimensions={1}, to_apply=%bitcast.103.reduce_sub_computation | reduce | bytes 1048578
  43.2 5.7 all-to-all-start.1
  49.6 7.1 %all-to-all-done.1 = bf16[8,2,16384]{2,1,0:T(2,128)(2,1)} async-done(((bf16[8,2,16384]{2,1,0:T(2,128)(2,1)}), bf16[8,2,16384]{2,1,0:T(2,128)(2,1)}, u32[]{:S(2)}, u32[]{:S(2)}) %all-to-all-start.1) | async-done | bytes 524320 | tf_op jit(solution)/shard_map/all_to_all | solution.py:115
  56.7 2.2 reshape.163
  62.1 11.5 %reduce.2 = bf16[2048,128]{1,0:T(8,128)(2,1)S(1)} reduce(bf16[2048,1,128]{2,1,0:T(2,128)(2,1)S(1)} %bitcast.152, bf16[]{:T(256)} %broadcast.51), dimensions={1}, to_apply=%bitcast.105.reduce_sub_computation | reduce | bytes 1048578
  73.7 17.9 %all_to_all.104 = bf16[8,2,16384]{2,1,0:T(2,128)(2,1)S(1)} all-to-all(bf16[8,2,16384]{2,1,0:T(2,128)(2,1)S(1)} %reshape.164), channel_id=1, replica_groups=mesh['seq'=32,'fsdp'=8] {'fsdp'}, dimensions={0} | all-to-all | bytes 1048576 | tf_op jit(solution)/shard_map/all_to_all | solution.py:113
  91.6 3.5 stack.2
  95.2 7.1 %all-to-all-start.2 = ((bf16[8,1,128,2048]{3,2,1,0:T(8,128)(2,1)}), bf16[8,1,128,2048]{3,2,1,0:T(8,128)(2,1)}, u32[]{:S(2)}, u32[]{:S(2)}) async-start(bf16[8,1,128,2048]{3,2,1,0:T(8,128)(2,1)} %stack.2), calls=%async_computation.2 | async-start | bytes 8388608 | tf_op jit(solution)/shard_map/all_to_all | solution.py:107
  102.9 55.7 %all-to-all-done.2 = bf16[8,1,128,2048]{3,2,1,0:T(8,128)(2,1)} async-done(((bf16[8,1,128,2048]{3,2,1,0:T(8,128)(2,1)}), bf16[8,1,128,2048]{3,2,1,0:T(8,128)(2,1)}, u32[]{:S(2)}, u32[]{:S(2)}) %all-to-all-start.2) | async-done | bytes 4194336 | tf_op jit(solution)/shard_map/all_to_all | solution.py:107
  158.6 3.4 fusion.20
  164.2 2.3 fusion.19
  166.5 2.3 fusion.18
  168.9 136.2 %all-gather.5.cloned.1.call-done = f32[256,2,128,128]{3,2,1,0:T(8,128)} async-done(((f32[8,2,128,128]{3,2,1,0:T(8,128)}), f32[256,2,128,128]{3,2,1,0:T(8,128)}) %all-gather.5.cloned.1.call-update) | async-done | bytes 33554448 | tf_op jit(solution)/shard_map/all_gather | solution.py:14
  305.1 51.9 %while.30 = (s32[]{:T(128)}, f32[8,2,128,128]{3,2,1,0:T(8,128)S(1)}, s32[]{:T(128)}, f32[32,8,2,128,128]{4,3,2,1,0:T(8,128)}, s32[]{:T(128)}, /*index=5*/s32[]{:T(128)}) while((s32[]{:T(128)}, f32[8,2,128,128]{3,2,1,0:T(8,128)S(1)}, s32[]{:T(128)}, f32[32,8,2,128,128]{4,3,2,1,0:T(8,128)}, s32[]{:T(128)}, /*index=5*/s32[]{:T(128)}) %tuple.90), condition=%wide.region_1.0_spmd.clone, body=%wide.region_0.0_spmd.clone.sunk | while | flops 786436 | bytes 3145829 | solution.py:23
  357.0 2.1 fusion.24
  360.8 4.9 fusion.4
  365.7 2.9 copy.108
  370.4 2.5 fusion.14
  372.9 5.7 all-to-all-start.3
  379.4 158.1 %all-gather.7.cloned.1.call-done = f32[256,2,128,128]{3,2,1,0:T(8,128)} async-done(((f32[8,2,128,128]{3,2,1,0:T(8,128)}), f32[256,2,128,128]{3,2,1,0:T(8,128)}) %all-gather.7.cloned.1.call-update) | async-done | bytes 33554448 | tf_op jit(solution)/shard_map/all_gather | solution.py:14
  537.5 52.3 %while.31 = (s32[]{:T(128)}, f32[8,2,128,128]{3,2,1,0:T(8,128)S(1)}, s32[]{:T(128)}, f32[32,8,2,128,128]{4,3,2,1,0:T(8,128)}, s32[]{:T(128)}, /*index=5*/s32[]{:T(128)}, s32[]{:T(128)}, s32[]{:T(128)}) while((s32[]{:T(128)}, f32[8,2,128,128]{3,2,1,0:T(8,128)S(1)}, s32[]{:T(128)}, f32[32,8,2,128,128]{4,3,2,1,0:T(8,128)}, s32[]{:T(128)}, ...), condition=%wide.region_3.4_spmd.clone, body=%wide.region_2.3_spmd.clone.sunk | while | flops 786440 | bytes 3145891 | solution.py:23
  593.2 2.3 fusion.17
  595.5 4.8 all-to-all-start.5
  602.1 2.1 fusion.15
  604.3 4.6 all-to-all-done.5
  608.9 5.5 all-to-all-start.6
  614.3 2.0 copy.105
  616.4 41.8 %reduce-scatter.4.cloned.1.call-done = f32[64,256]{1,0:T(8,128)} async-done(((f32[2048,256]{1,0:T(8,128)}), f32[64,256]{1,0:T(8,128)}) %reduce-scatter.4.cloned.1.call-update) | async-done | bytes 65552
  (120 shorter events, 125.4 us)
Async XLA Ops:
  7.2 151.4 %copy-start = (bf16[2048,256]{1,0:T(8,128)(2,1)S(1)}, bf16[2048,256]{1,0:T(8,128)(2,1)}, u32[]{:S(2)}) copy-start(bf16[2048,256]{1,0:T(8,128)(2,1)} %param.13) | copy-start | bytes 3145732
  22.6 20.6 %all-to-all-start = ((bf16[8,2,16384]{2,1,0:T(2,128)(2,1)}), bf16[8,2,16384]{2,1,0:T(2,128)(2,1)S(1)}, u32[]{:S(2)}, u32[]{:S(2)}) async-start(bf16[8,2,16384]{2,1,0:T(2,128)(2,1)} %reshape.160), calls=%async_computation | async-start | bytes 1048576 | tf_op jit(solution)/shard_map/all_to_all | solution.py:114
  43.2 13.5 %all-to-all-start.1 = ((bf16[8,2,16384]{2,1,0:T(2,128)(2,1)}), bf16[8,2,16384]{2,1,0:T(2,128)(2,1)}, u32[]{:S(2)}, u32[]{:S(2)}) async-start(bf16[8,2,16384]{2,1,0:T(2,128)(2,1)} %reshape.162), calls=%async_computation.1 | async-start | bytes 1048576 | tf_op jit(solution)/shard_map/all_to_all | solution.py:115
  48.9 256.1 %all-gather.5.cloned.1.call-start = ((), (), s32[]{:S(2)}) async-start(), calls=%async_computation.8 | async-start | bytes 34603008 | tf_op jit(solution)/shard_map/all_gather | solution.py:14
  49.5 11.8 %copy-start.9 = (bf16[1,128,2048]{2,1,0:T(8,128)(2,1)S(1)}, bf16[1,128,2048]{2,1,0:T(8,128)(2,1)}, u32[]{:S(2)}) copy-start(bf16[1,128,2048]{2,1,0:T(8,128)(2,1)} %param.9) | copy-start | bytes 1572868
  49.6 24.0 %copy-start.2 = (bf16[1,128,2048]{1,2,0:T(8,128)(2,1)}, bf16[1,128,2048]{1,2,0:T(8,128)(2,1)S(1)}, u32[]{:S(2)}) copy-start(bf16[1,128,2048]{1,2,0:T(8,128)(2,1)S(1)} %copy.110) | copy-start | bytes 1572868
  59.0 0.8 copy-start.4
  95.2 63.4 %all-to-all-start.2 = ((bf16[8,1,128,2048]{3,2,1,0:T(8,128)(2,1)}), bf16[8,1,128,2048]{3,2,1,0:T(8,128)(2,1)}, u32[]{:S(2)}, u32[]{:S(2)}) async-start(bf16[8,1,128,2048]{3,2,1,0:T(8,128)(2,1)} %stack.2), calls=%async_computation.2 | async-start | bytes 8388608 | tf_op jit(solution)/shard_map/all_to_all | solution.py:107
  102.3 435.2 %all-gather.7.cloned.1.call-start = ((), (), s32[]{:S(2)}) async-start(), calls=%async_computation.9 | async-start | bytes 34603008 | tf_op jit(solution)/shard_map/all_gather | solution.py:14
  102.9 59.4 %copy-start.6 = (bf16[1,128,2048]{1,2,0:T(8,128)(2,1)}, bf16[1,128,2048]{1,2,0:T(8,128)(2,1)S(1)}, u32[]{:S(2)}) copy-start(bf16[1,128,2048]{1,2,0:T(8,128)(2,1)S(1)} %copy.112) | copy-start | bytes 1572868
  162.3 1.8 copy-start.7
  372.9 222.6 %all-to-all-start.3 = ((bf16[8,128,256]{1,2,0:T(8,128)(2,1)}), bf16[8,128,256]{1,2,0:T(8,128)(2,1)}, u32[]{:S(2)}, u32[]{:S(2)}) async-start(bf16[8,128,256]{1,2,0:T(8,128)(2,1)} %bitcast.13), calls=%async_computation.3 | async-start | bytes 1048576 | tf_op jit(solution)/shard_map/all_to_all | solution.py:125
  378.7 279.5 %reduce-scatter.4.cloned.1.call-start = ((), (), s32[]{:S(2)}) async-start(), calls=%async_computation.10 | async-start | bytes 2162688
  537.5 53.6 %copy-start.5 = (bf16[1,128,2048]{1,2,0:T(8,128)(2,1)S(1)}, bf16[1,128,2048]{1,2,0:T(8,128)(2,1)}, u32[]{:S(2)}) copy-start(bf16[1,128,2048]{1,2,0:T(8,128)(2,1)} %copy-done.4) | copy-start | bytes 1572868
  591.1 9.2 %copy-start.3 = (bf16[1,128,2048]{1,2,0:T(8,128)(2,1)S(1)}, bf16[1,128,2048]{1,2,0:T(8,128)(2,1)}, u32[]{:S(2)}) copy-start(bf16[1,128,2048]{1,2,0:T(8,128)(2,1)} %copy-done.2) | copy-start | bytes 1572868
  593.2 9.0 %copy-start.8 = (bf16[8,128,256]{1,2,0:T(8,128)(2,1)S(1)}, bf16[8,128,256]{1,2,0:T(8,128)(2,1)}, u32[]{:S(2)}) copy-start(bf16[8,128,256]{1,2,0:T(8,128)(2,1)} %copy-done.7) | copy-start | bytes 1572868
  595.5 13.4 %all-to-all-start.5 = ((bf16[8,128,256]{1,2,0:T(8,128)(2,1)}), bf16[8,128,256]{1,2,0:T(8,128)(2,1)}, u32[]{:S(2)}, u32[]{:S(2)}) async-start(bf16[8,128,256]{1,2,0:T(8,128)(2,1)} %bitcast.154), calls=%async_computation.5 | async-start | bytes 1048576 | tf_op jit(solution)/shard_map/all_to_all | solution.py:128
  600.4 62.5 %copy-start.1 = (bf16[2048,256]{1,0:T(8,128)(2,1)S(1)}, bf16[2048,256]{1,0:T(8,128)(2,1)}, u32[]{:S(2)}) copy-start(bf16[2048,256]{1,0:T(8,128)(2,1)} %param.13) | copy-start | bytes 3145732
  608.9 53.0 %all-to-all-start.6 = ((bf16[8,128,256]{1,2,0:T(8,128)(2,1)}), bf16[8,128,256]{1,2,0:T(8,128)(2,1)S(1)}, u32[]{:S(2)}, u32[]{:S(2)}) async-start(bf16[8,128,256]{1,2,0:T(8,128)(2,1)} %bitcast.31), calls=%async_computation.6 | async-start | bytes 1048576 | tf_op jit(solution)/shard_map/all_to_all | solution.py:131
Sparse Core Ops, SparseCore 0:
  61.4 243.6 all-gather.4
  307.9 229.6 all-gather.6
  541.7 116.4 reduce-scatter.3
